TPU v7x, 512 devices: a whole 4x4x16 slice. The times are simulated.
512 devices in a mesh: seq: 64 (over z, y), tp: 8 (over x, core).
Axes of the slice: x: 4, y: 4, z: 16, core: 2. Of those that a mesh axis runs over, the one named last changes fastest.
Arguments:
- hidden: bfloat16 [384, 2048], P(None, 'seq'), may hold values from -12 to 12
- ln1_gain: float32 [2048], P('seq'), may hold values from 0.1 to 1.9
- wq: bfloat16 [2048, 2048], P('seq', 'tp'), may hold values from -0.125 to 0.125
- wk: bfloat16 [2048, 1024], P('seq', 'tp'), may hold values from -0.125 to 0.125
- wv: bfloat16 [2048, 1024], P('seq', 'tp'), may hold values from -0.125 to 0.125
- wg: bfloat16 [2048, 2048], P('seq', 'tp'), may hold values from -0.125 to 0.125
- q_gain: float32 [128], replicated, may hold values from 1 to 30
- key_gain: float32 [128], replicated, may hold values from 0.5 to 1.5
- wo: bfloat16 [2048, 2048], P('tp', 'seq'), may hold values from -0.5 to 0.5
- ln2_gain: float32 [2048], P('seq'), may hold values from 0.1 to 1.9
- w_gate: bfloat16 [2048, 6144], P('seq', 'tp'), may hold values from -0.125 to 0.125
- w_up: bfloat16 [2048, 6144], P('seq', 'tp'), may hold values from -0.125 to 0.125
- w_down: bfloat16 [6144, 2048], P('tp', 'seq'), may hold values from -0.078125 to 0.078125
- last_gain: float32 [2048], P('seq'), may hold values from 0.1 to 1.9
- head_weight: bfloat16 [2048, 131072], P(None, ('seq', 'tp')), may hold values from -0.125 to 0.125
- inv_temp: float32 [8], replicated, may hold values from 0.5 to 64
- key_cache: bfloat16 [8, 16384, 1024], P(None, 'seq', 'tp'), may hold values from -40 to 40
- value_cache: bfloat16 [8, 16384, 1024], P(None, 'seq', 'tp'), may hold values from -6 to 6
- lengths: int32 [8], replicated, may hold values from 1 to 16336
- parents: int32 [8, 48], replicated, may hold values from 0 to 46, as said below
- accepted: int32 [8], replicated, may hold values from 0 to 47
Outputs:
- logprobs: float32 [384, 131072], P(None, ('seq', 'tp'))
- next_hidden: bfloat16 [384, 2048], P(None, 'seq')
- updated_key_cache: bfloat16 [8, 16384, 1024], P(None, 'seq', 'tp')
- updated_value_cache: bfloat16 [8, 16384, 1024], P(None, 'seq', 'tp')
Inputs may be any that keep to these rules, and one draw needn't show every extreme that they name: parents[r, 0] = 0; for i >= 1, i - 4 <= parents[r, i] < i.
All inputs are finite; a program needn't handle non-finite values.
Results may differ from a plain program's by a relative error of at most 0.012.
Values may be sent and summed in bfloat16 or wider, within the bound.
No kernel may reach another device: no remote copies, remote signals or barrier semaphores. Data moves between devices by JAX's collectives and lax.ppermute only.
A program may use at most 128 MiB of HBM per device.

v0:
```python
import jax
import jax.numpy as jnp
from jax import lax
from jax.sharding import PartitionSpec as P

EPSILON = 1e-06
ROPE_BASE = 1000000.0
NEGATIVE = -1e30


def ancestry(parents):
    node_count = parents.shape[-1]
    node_ids = jnp.arange(node_count, dtype=jnp.int32)
    reachable = (parents[..., :, None] == node_ids[None, :]).astype(jnp.float32)
    reachable = jnp.maximum(reachable, jnp.eye(node_count, dtype=jnp.float32))
    for turn in range((node_count - 1).bit_length()):
        reachable = jnp.minimum(
            jnp.einsum("rij,rjk->rik", reachable, reachable, precision=lax.Precision.HIGHEST), 1.0
        )
    return reachable


def head_norm(values, gain):
    meansq = jnp.mean(values * values, axis=-1, keepdims=True)
    return values * lax.rsqrt(meansq + EPSILON) * gain


def apply_rotary(values, places):
    half_dim = values.shape[-1] // 2
    spread = ROPE_BASE ** (-jnp.arange(half_dim, dtype=jnp.float32) / half_dim)
    angles = places.astype(jnp.float32)[:, None] * spread[None, :]
    cosine = jnp.cos(angles)[:, None, :]
    sine = jnp.sin(angles)[:, None, :]
    lower_part = values[..., :half_dim]
    upper_part = values[..., half_dim:]
    return jnp.concatenate(
        [lower_part * cosine - upper_part * sine, upper_part * cosine + lower_part * sine], axis=-1
    )


def cache_part(query_blocks, key_block, value_block, valid_slot):
    scores = jnp.einsum(
        "rikgd,rckd->rkgic", query_blocks, key_block, preferred_element_type=jnp.float32
    )
    valid_slot = valid_slot[:, None, None, None, :]
    row_peak = jnp.max(jnp.where(valid_slot, scores, NEGATIVE), axis=-1)
    weights = jnp.where(valid_slot, jnp.exp(scores - row_peak[..., None]), 0.0)
    row_mass = jnp.sum(weights, axis=-1)
    weighted = jnp.einsum(
        "rkgic,rckd->rkgid",
        weights.astype(jnp.bfloat16),
        value_block,
        preferred_element_type=jnp.float32,
    )
    return (row_peak, row_mass, weighted)


def on_device(
    hidden,
    ln1_gain,
    wq,
    wk,
    wv,
    wg,
    q_gain,
    key_gain,
    wo,
    ln2_gain,
    w_gate,
    w_up,
    w_down,
    last_gain,
    head_weight,
    inv_temp,
    key_cache,
    value_cache,
    lengths,
    parents,
    accepted,
):
    seq_count = lax.axis_size("seq")
    model_width = hidden.shape[1] * seq_count
    head_dim = q_gain.shape[0]
    query_heads = wq.shape[1] // head_dim
    kv_heads = wk.shape[1] // head_dim
    query_group_size = query_heads // kv_heads
    requests, tree_size = parents.shape
    token_count = hidden.shape[0]
    slot_count = key_cache.shape[1]
    slot_start = lax.axis_index("seq") * slot_count
    parent_links = ancestry(parents)
    tree_node_depth = jnp.sum((parent_links > 0.5).astype(jnp.int32), axis=-1) - 1
    token_position = (lengths[:, None] + tree_node_depth).reshape(-1)
    hidden_wide = hidden.astype(jnp.float32)
    squares = lax.psum(jnp.sum(hidden_wide * hidden_wide, axis=1), "seq")
    normed1 = (hidden_wide * lax.rsqrt(squares / model_width + EPSILON)[:, None] * ln1_gain).astype(
        jnp.bfloat16
    )
    q_sum, key_sum, v_sum, gate = lax.psum(
        (
            jnp.dot(normed1, wq, preferred_element_type=jnp.float32),
            jnp.dot(normed1, wk, preferred_element_type=jnp.float32),
            jnp.dot(normed1, wv, preferred_element_type=jnp.float32),
            jnp.dot(normed1, wg, preferred_element_type=jnp.float32),
        ),
        "seq",
    )
    query_rows_all = apply_rotary(
        head_norm(q_sum.reshape(token_count, query_heads, head_dim), q_gain), token_position
    ) * head_dim ** (-0.5)
    query_rows_all = query_rows_all.astype(jnp.bfloat16).reshape(
        requests, tree_size, kv_heads, query_group_size, head_dim
    )
    draft_keys = apply_rotary(
        head_norm(key_sum.reshape(token_count, kv_heads, head_dim), key_gain), token_position
    ).astype(jnp.bfloat16)
    draft_values = v_sum.astype(jnp.bfloat16)
    tree_keys = draft_keys.reshape(requests, tree_size, kv_heads, head_dim)
    tree_values = draft_values.reshape(requests, tree_size, kv_heads, head_dim)
    cache_keys = key_cache.reshape(requests, slot_count, kv_heads, head_dim)
    cache_values = value_cache.reshape(requests, slot_count, kv_heads, head_dim)
    slot_ids = slot_start + jnp.arange(slot_count, dtype=jnp.int32)
    local_state = cache_part(
        query_rows_all, cache_keys, cache_values, slot_ids[None, :] < lengths[:, None]
    )
    local_peak, local_mass, local_sum = local_state
    cache_peak = lax.pmax(local_peak, "seq")
    factor = jnp.exp(local_peak - cache_peak)
    cache_mass, cache_sum = lax.psum((local_mass * factor, local_sum * factor[..., None]), "seq")
    tree_scores = jnp.einsum(
        "rikgd,rjkd->rkgij", query_rows_all, tree_keys, preferred_element_type=jnp.float32
    )
    valid_node = (parent_links > 0.5)[:, None, None, :, :]
    row_top = jnp.maximum(
        cache_peak, jnp.max(jnp.where(valid_node, tree_scores, NEGATIVE), axis=-1)
    )
    tree_weights = jnp.where(valid_node, jnp.exp(tree_scores - row_top[..., None]), 0.0)
    cache_factor = jnp.exp(cache_peak - row_top)
    row_mass = cache_mass * cache_factor + jnp.sum(tree_weights, axis=-1)
    weighted = cache_sum * cache_factor[..., None] + jnp.einsum(
        "rkgij,rjkd->rkgid",
        tree_weights.astype(jnp.bfloat16),
        tree_values,
        preferred_element_type=jnp.float32,
    )
    attention_result = jnp.transpose(weighted / row_mass[..., None], (0, 3, 1, 2, 4)).reshape(
        token_count, query_heads * head_dim
    )
    gated = (attention_result * jax.nn.sigmoid(gate)).astype(jnp.bfloat16)
    attn_sum = lax.psum(jnp.dot(gated, wo, preferred_element_type=jnp.float32), "tp")
    middle = (hidden_wide + attn_sum).astype(jnp.bfloat16)
    middle_wide = middle.astype(jnp.float32)
    squares_mid = lax.psum(jnp.sum(middle_wide * middle_wide, axis=1), "seq")
    normed2 = (
        middle_wide * lax.rsqrt(squares_mid / model_width + EPSILON)[:, None] * ln2_gain
    ).astype(jnp.bfloat16)
    gate_part, up_part = lax.psum(
        (
            jnp.dot(normed2, w_gate, preferred_element_type=jnp.float32),
            jnp.dot(normed2, w_up, preferred_element_type=jnp.float32),
        ),
        "seq",
    )
    activated = (jax.nn.silu(gate_part) * up_part).astype(jnp.bfloat16)
    down_part = jnp.dot(activated, w_down, preferred_element_type=jnp.float32)
    down_sum = lax.psum(down_part, "tp")
    next_hidden = (middle_wide + down_sum).astype(jnp.bfloat16)
    next_wide = next_hidden.astype(jnp.float32)
    squares_last = lax.psum(jnp.sum(next_wide * next_wide, axis=1), "seq")
    normed3 = (
        next_wide * lax.rsqrt(squares_last / model_width + EPSILON)[:, None] * last_gain
    ).astype(jnp.bfloat16)
    logits = jnp.dot(
        lax.all_gather(normed3, "seq", axis=1, tiled=True),
        head_weight,
        preferred_element_type=jnp.float32,
    )
    logits = logits * jnp.repeat(inv_temp, tree_size)[:, None]
    vocab_top = lax.pmax(jnp.max(logits, axis=1), ("seq", "tp"))
    vocab_total = lax.psum(jnp.sum(jnp.exp(logits - vocab_top[:, None]), axis=1), ("seq", "tp"))
    logprobs = logits - (vocab_top + jnp.log(vocab_total))[:, None]
    accepted_rows = parent_links[jnp.arange(requests), accepted]
    target = token_position.reshape(requests, tree_size)
    slot_all = slot_start + jnp.arange(slot_count, dtype=jnp.int32)
    placed = (slot_all[None, :, None] == target[:, None, :]).astype(jnp.float32) * accepted_rows[
        :, None, :
    ]
    hits = (jnp.sum(placed, axis=2) > 0.5)[:, :, None]
    placed_low = placed.astype(jnp.bfloat16)
    moved_keys = jnp.einsum(
        "rca,rae->rce",
        placed_low,
        draft_keys.reshape(requests, tree_size, kv_heads * head_dim),
        preferred_element_type=jnp.float32,
    ).astype(jnp.bfloat16)
    moved_values = jnp.einsum(
        "rca,rae->rce",
        placed_low,
        draft_values.reshape(requests, tree_size, kv_heads * head_dim),
        preferred_element_type=jnp.float32,
    ).astype(jnp.bfloat16)
    updated_key_cache = jnp.where(hits, moved_keys, key_cache)
    updated_value_cache = jnp.where(hits, moved_values, value_cache)
    return (logprobs, next_hidden, updated_key_cache, updated_value_cache)


def solution(mesh):
    in_specs = (
        P(None, "seq"),
        P("seq"),
        P("seq", "tp"),
        P("seq", "tp"),
        P("seq", "tp"),
        P("seq", "tp"),
        P(),
        P(),
        P("tp", "seq"),
        P("seq"),
        P("seq", "tp"),
        P("seq", "tp"),
        P("tp", "seq"),
        P("seq"),
        P(None, ("seq", "tp")),
        P(),
        P(None, "seq", "tp"),
        P(None, "seq", "tp"),
        P(),
        P(),
        P(),
    )
    out_specs = (P(None, ("seq", "tp")), P(None, "seq"), P(None, "seq", "tp"), P(None, "seq", "tp"))
    return jax.shard_map(
        on_device, mesh=mesh, in_specs=in_specs, out_specs=out_specs, check_vma=False
    )
```

profile of v0, /device:TPU:1, one launch (start us, length us, event | category | flops | bytes accessed | tf_op | source)
XLA Modules:
  0.0 1792.0 jit_solution(4256023891018787633)
XLA Ops:
  7.2 0.8 fusion.51
  8.1 122.9 %psum.98 = f32[384]{0:T(512)S(1)} all-reduce(f32[384]{0:T(512)S(1)} %fusion.51), channel_id=1, replica_groups=mesh['seq'=64,'tp'=8] {'seq'}, use_global_device_ids=true, to_apply=%region_1.0 | all-reduce | flops 384 | bytes 3072 | tf_op jit(solution)/shard_map/psum | solution.py:95
  130.9 1.8 fusion.88
  132.8 1.4 convolution_minimum_fusion.5
  136.2 1.0 fusion.86
  137.7 1.1 fusion.82
  138.7 269.0 %all-reduce.8.cloned.1.call-done = f32[384,2,128]{0,2,1:T(8,128)} async-done(((f32[384,2,128]{0,2,1:T(8,128)}), f32[384,2,128]{0,2,1:T(8,128)}) %all-reduce.8.cloned.1.call-update) | async-done | bytes 393232 | tf_op jit(solution)/shard_map/psum | solution.py:99
  407.7 1.0 multiply_reduce_fusion
  408.8 1.1 multiply_multiply_fusion
  411.8 114.2 %pmax.14 = f32[8,1,2,48]{3,2,0,1:T(2,128)S(1)} all-reduce(f32[8,1,2,48]{3,2,0,1:T(2,128)S(1)} %bitcast.134), channel_id=1, replica_groups=mesh['seq'=64,'tp'=8] {'seq'}, use_global_device_ids=true, to_apply=%region_6.0 | all-reduce | flops 768 | bytes 6144 | tf_op jit(solution)/shard_map/pmax | solution.py:127
  526.5 1.1 fusion.2
  528.0 219.4 %all-reduce.13 = (bf16[384,128]{1,0:T(8,128)(2,1)S(1)}, f32[8,1,2,48]{3,2,0,1:T(2,128)S(1)}) all-reduce(f32[384,128]{1,0:T(8,128)S(1)} %fusion.84, f32[8,1,2,48]{3,2,0,1:T(2,128)S(1)} %get-tuple-element.32), channel_id=1, replica_groups=mesh['seq'=64,'tp'=8] {'seq'}, use_global_device_ids=true, to_apply=%region_11.12 | all-reduce | flops 49920 | bytes 301056 | tf_op jit(solution)/shard_map/psum | solution.py:99
  747.3 74.5 %all-reduce.12.cloned.1.call-done = (f32[8,1,2,48,128]{4,3,2,0,1:T(8,128)}, f32[384,128]{1,0:T(8,128)}, f32[384,256]{1,0:T(8,128)}) async-done(((f32[8,1,2,48,128]{4,3,2,0,1:T(8,128)}, f32[384,128]{1,0:T(8,128)}, f32[384,256]{1,0:T(8,128)}), (f32[8,1,2,48,128]{4,3,2,0,1:T(8,128)}, f32[384,128]{1,0:T(8,128)}, f32[384,256]{1,0:T(8,128)})) %all-reduce.12.cloned.1.call-update) | async-done | bytes 983056 | tf_op jit(solution)/shard_map/psum | solution.py:129
  821.8 1.1 multiply_reduce_fusion.1
  822.9 1.1 multiply_bitcast_fusion
  824.0 0.8 fusion.25
  826.7 39.8 %psum.105 = f32[384,32]{0,1:T(8,128)S(1)} all-reduce(f32[384,32]{0,1:T(8,128)S(1)} %fusion.43), channel_id=1, replica_groups=mesh['seq'=64,'tp'=8] {'tp'}, use_global_device_ids=true, to_apply=%region_16.17 | all-reduce | flops 12288 | bytes 98304 | tf_op jit(solution)/shard_map/psum | solution.py:150
  866.5 110.1 %psum.106 = f32[384]{0:T(512)S(1)} all-reduce(f32[384]{0:T(512)S(1)} %get-tuple-element.21), channel_id=1, replica_groups=mesh['seq'=64,'tp'=8] {'seq'}, use_global_device_ids=true, to_apply=%region_18.19 | all-reduce | flops 384 | bytes 3072 | tf_op jit(solution)/shard_map/psum | solution.py:153
  976.7 1.4 fusion.63
  978.1 1.4 fusion.65
  979.6 295.4 %all-reduce.10.cloned.1.call-done = (f32[384,768]{1,0:T(8,128)}, f32[384,768]{1,0:T(8,128)}) async-done(((f32[384,768]{1,0:T(8,128)}, f32[384,768]{1,0:T(8,128)}), (f32[384,768]{1,0:T(8,128)}, f32[384,768]{1,0:T(8,128)})) %all-reduce.10.cloned.1.call-update) | async-done | bytes 2359312 | tf_op jit(solution)/shard_map/psum | solution.py:157
  1275.1 2.1 fusion.8
  1277.2 30.1 %psum.109 = f32[384,32]{0,1:T(8,128)S(1)} all-reduce(f32[384,32]{0,1:T(8,128)S(1)} %fusion.8), channel_id=1, replica_groups=mesh['seq'=64,'tp'=8] {'tp'}, use_global_device_ids=true, to_apply=%region_21.22 | all-reduce | flops 12288 | bytes 98304 | tf_op jit(solution)/shard_map/psum | solution.py:166
  1307.3 112.8 %psum.110 = f32[384]{0:T(512)S(1)} all-reduce(f32[384]{0:T(512)S(1)} %get-tuple-element.19), channel_id=1, replica_groups=mesh['seq'=64,'tp'=8] {'seq'}, use_global_device_ids=true, to_apply=%region_23.24 | all-reduce | flops 384 | bytes 3072 | tf_op jit(solution)/shard_map/psum | solution.py:169
  1420.1 0.7 fusion.50
  1421.9 1.7 fusion.1
  1423.5 1.6 fusion
  1425.1 148.8 %all-gather.2.cloned.1.call-done = bf16[384,2048]{0,1:T(8,128)(2,1)} async-done(((bf16[384,32]{0,1:T(8,128)(2,1)}), bf16[384,2048]{0,1:T(8,128)(2,1)}) %all-gather.2.cloned.1.call-update) | async-done | bytes 1572880 | tf_op jit(solution)/shard_map/all_gather | solution.py:174
  1573.9 2.2 fusion.93
  1576.1 109.6 %pmax.15 = f32[384]{0:T(512)S(1)} all-reduce(f32[384]{0:T(512)S(1)} %get-tuple-element.41), channel_id=1, replica_groups=mesh['seq'=64,'tp'=8] {'seq','tp'}, use_global_device_ids=true, to_apply=%region_25.26 | all-reduce | flops 384 | bytes 3072 | tf_op jit(solution)/shard_map/pmax | solution.py:179
  1685.8 98.8 %psum.111 = f32[384]{0:T(512)S(1)} all-reduce(f32[384]{0:T(512)S(1)} %exponential_reduce_fusion), channel_id=1, replica_groups=mesh['seq'=64,'tp'=8] {'seq','tp'}, use_global_device_ids=true, to_apply=%region_27.28 | all-reduce | flops 384 | bytes 3072 | tf_op jit(solution)/shard_map/psum | solution.py:180
  1784.6 0.9 copy.35
  (100 shorter events, 8.2 us)
Async XLA Ops:
  7.2 1566.7 %copy-start = (bf16[2048,256]{1,0:T(8,128)(2,1)S(1)}, bf16[2048,256]{1,0:T(8,128)(2,1)}, u32[]{:S(2)}) copy-start(bf16[2048,256]{1,0:T(8,128)(2,1)} %param.35) | copy-start | bytes 3145732
  7.2 400.6 %all-reduce.8.cloned.1.call-start = ((), (), s32[]{:S(2)}) async-start(), calls=%async_computation | async-start | bytes 786432 | tf_op jit(solution)/shard_map/psum | solution.py:99
  132.7 689.1 %all-reduce.12.cloned.1.call-start = ((), (), s32[]{:S(2)}) async-start(), calls=%async_computation.3 | async-start | bytes 1966080 | tf_op jit(solution)/shard_map/psum | solution.py:129
  134.6 1.4 copy-start.12
  134.6 1.6 copy-start.1
  134.6 1.6 copy-start.8
  134.6 1.6 copy-start.9
  135.0 2.7 copy-start.7
  135.3 273.5 %copy-start.16 = (f32[128]{0:T(128)S(1)}, f32[128]{0:T(128)}, u32[]{:S(2)}) copy-start(f32[128]{0:T(128)} %param.27) | copy-start | bytes 1540
  410.4 1.0 copy-start.2
  411.4 115.0 %copy-start.3 = (bf16[8,256,128]{2,1,0:T(8,128)(2,1)S(1)}, bf16[8,256,128]{2,1,0:T(8,128)(2,1)}, u32[]{:S(2)}) copy-start(bf16[8,256,128]{2,1,0:T(8,128)(2,1)} %param.38) | copy-start | bytes 1572868
  526.5 1.2 copy-start.10
  527.6 295.3 %copy-start.13 = (f32[128]{0:T(128)S(1)}, f32[128]{0:T(128)}, u32[]{:S(2)}) copy-start(f32[128]{0:T(128)} %param.28) | copy-start | bytes 1540
  527.6 747.5 %all-reduce.10.cloned.1.call-start = ((), (), s32[]{:S(2)}) async-start(), calls=%async_computation.2 | async-start | bytes 4718592 | tf_op jit(solution)/shard_map/psum | solution.py:157
  822.9 2.5 copy-start.18
  825.4 1.0 copy-start.17
  825.4 1.0 copy-start.20
  826.0 150.7 %copy-start.5 = (bf16[32,768]{1,0:T(8,128)(2,1)S(1)}, bf16[32,768]{1,0:T(8,128)(2,1)}, u32[]{:S(2)}) copy-start(bf16[32,768]{1,0:T(8,128)(2,1)} %param.32) | copy-start | bytes 147460
  826.0 150.7 %copy-start.11 = (f32[32]{0:T(128)S(1)}, f32[32]{0:T(128)}, u32[]{:S(2)}) copy-start(f32[32]{0:T(128)} %param.30) | copy-start | bytes 388
  826.7 151.5 %copy-start.6 = (bf16[32,768]{1,0:T(8,128)(2,1)S(1)}, bf16[32,768]{1,0:T(8,128)(2,1)}, u32[]{:S(2)}) copy-start(bf16[32,768]{1,0:T(8,128)(2,1)} %param.31) | copy-start | bytes 147460
  979.5 295.5 %copy-start.19 = (bf16[768,32]{0,1:T(8,128)(2,1)S(1)}, bf16[768,32]{0,1:T(8,128)(2,1)}, u32[]{:S(2)}) copy-start(bf16[768,32]{0,1:T(8,128)(2,1)} %param.33) | copy-start | bytes 147460
  979.6 594.3 %all-gather.2.cloned.1.call-start = ((), (), s32[]{:S(2)}) async-start(), calls=%async_computation.1 | async-start | bytes 1597440 | tf_op jit(solution)/shard_map/all_gather | solution.py:174
  1275.0 145.0 %copy-start.14 = (f32[32]{0:T(128)S(1)}, f32[32]{0:T(128)}, u32[]{:S(2)}) copy-start(f32[32]{0:T(128)} %param.34) | copy-start | bytes 388
  1275.0 145.7 %copy-start.15 = (f32[8]{0:T(128)S(1)}, f32[8]{0:T(128)}, u32[]{:S(2)}) copy-start(f32[8]{0:T(128)} %param.36) | copy-start | bytes 100
  1275.0 146.0 %copy-start.21 = (s32[8]{0:T(128)S(1)}, s32[8]{0:T(128)}, u32[]{:S(2)}) copy-start(s32[8]{0:T(128)} %param.41) | copy-start | bytes 100
  1307.3 117.8 %copy-start.4 = (bf16[384,32]{0,1:T(8,128)(2,1)}, bf16[384,32]{0,1:T(8,128)(2,1)S(1)}, u32[]{:S(2)}) copy-start(bf16[384,32]{0,1:T(8,128)(2,1)S(1)} %get-tuple-element.20) | copy-start | bytes 73732
Sparse Core Ops, SparseCore 0:
  132.9 274.8 all-reduce.7
  527.7 294.0 all-reduce.11
  979.7 295.2 all-reduce.9
  1420.9 152.9 all-gather.1
where the time goes:
time: 1790 us
  blocking collectives  958 us (54%)
  waiting for transfers between devices  788 us (44%)
  matrix products  19.9 us (1%)
    psum x1, waiting for transfers between devices, on_device(): lax.psum((jnp.dot(normed2, w_gate, preferred_element_type=jnp.float32), j...  295 us
    psum x1, waiting for transfers between devices, on_device(): lax.psum((jnp.dot(normed1, wq, preferred_element_type=jnp.float32), jnp.d...  269 us
    psum x1, blocking collectives, on_device(): lax.psum((jnp.dot(normed1, wq, preferred_element_type=jnp.float32), jnp.d...  219 us
    all_gather x1, waiting for transfers between devices, on_device(): lax.all_gather(normed3, 'seq', axis=1, tiled=True)  149 us
    psum x1, blocking collectives, on_device(): squares = lax.psum(jnp.sum(hidden_wide * hidden_wide, axis=1), 'seq')  123 us
    pmax x1, blocking collectives, on_device(): cache_peak = lax.pmax(local_peak, 'seq')  114 us
    psum x1, blocking collectives, on_device(): squares_last = lax.psum(jnp.sum(next_wide * next_wide, axis=1), 'seq')  113 us
    psum x1, blocking collectives, on_device(): squares_mid = lax.psum(jnp.sum(middle_wide * middle_wide, axis=1), 'seq')  110 us
  transfers between devices with their start and end apart: 4, of which 4 were waited for; matrix products, arithmetic and copies ran while one was open for 1% of the time, Pallas kernels for 0%

commit v1 on v0

--- a/solution.py
+++ b/solution.py
@@ -171,7 +171,9 @@
         next_wide * lax.rsqrt(squares_last / model_width + EPSILON)[:, None] * last_gain
     ).astype(jnp.bfloat16)
     logits = jnp.dot(
-        lax.all_gather(normed3, "seq", axis=1, tiled=True),
+        jnp.concatenate(
+            lax.all_to_all(jnp.stack([normed3] * lax.axis_size("seq")), "seq", 0, 0), axis=1
+        ),
         head_weight,
         preferred_element_type=jnp.float32,
     )

time: 1790 us -> 1720 us (0.961)
  waiting for transfers between devices: 788 us -> 676 us
  blocking collectives: 958 us -> 985 us
    all_gather x1 -> x0, waiting for transfers between devices: 149 us -> none  [on_device(): lax.all_gather(normed3, 'seq', axis=1, tiled=True)]
    all_to_all x0 -> x1, waiting for transfers between devices: none -> 36.7 us  [on_device(): lax.all_to_all(jnp.stack([normed3] * lax.axis_size('seq')), 'seq', 0, 0)]
    pmax x1, blocking collectives: 110 us -> 136 us  [on_device(): vocab_top = lax.pmax(jnp.max(logits, axis=1), ('seq', 'tp'))]
where the time goes in v1:
time: 1720 us
  blocking collectives  985 us (57%)
  waiting for transfers between devices  676 us (39%)
  matrix products  19.4 us (1%)
    psum x1, waiting for transfers between devices, on_device(): lax.psum((jnp.dot(normed2, w_gate, preferred_element_type=jnp.float32), j...  295 us
    psum x1, waiting for transfers between devices, on_device(): lax.psum((jnp.dot(normed1, wq, preferred_element_type=jnp.float32), jnp.d...  269 us
    psum x1, blocking collectives, on_device(): lax.psum((jnp.dot(normed1, wq, preferred_element_type=jnp.float32), jnp.d...  219 us
    pmax x1, blocking collectives, on_device(): vocab_top = lax.pmax(jnp.max(logits, axis=1), ('seq', 'tp'))  136 us
    psum x1, blocking collectives, on_device(): squares = lax.psum(jnp.sum(hidden_wide * hidden_wide, axis=1), 'seq')  123 us
    pmax x1, blocking collectives, on_device(): cache_peak = lax.pmax(local_peak, 'seq')  114 us
    psum x1, blocking collectives, on_device(): squares_last = lax.psum(jnp.sum(next_wide * next_wide, axis=1), 'seq')  113 us
    psum x1, blocking collectives, on_device(): squares_mid = lax.psum(jnp.sum(middle_wide * middle_wide, axis=1), 'seq')  110 us
  transfers between devices with their start and end apart: 4, of which 4 were waited for; matrix products, arithmetic and copies ran while one was open for 1% of the time, Pallas kernels for 0%

profile of v1, /device:TPU:1, one launch (start us, length us, event | category | flops | bytes accessed | tf_op | source)
XLA Modules:
  0.0 1717.7 jit_solution(9531586859415638643)
XLA Ops:
  7.2 0.8 fusion.51
  8.1 122.9 %psum.98 = f32[384]{0:T(512)S(1)} all-reduce(f32[384]{0:T(512)S(1)} %fusion.51), channel_id=1, replica_groups=mesh['seq'=64,'tp'=8] {'seq'}, use_global_device_ids=true, to_apply=%region_1.0 | all-reduce | flops 384 | bytes 3072 | tf_op jit(solution)/shard_map/psum | solution.py:95
  130.9 1.8 fusion.88
  132.8 1.4 convolution_minimum_fusion.5
  136.2 1.0 fusion.86
  137.7 1.1 fusion.82
  138.7 269.0 %all-reduce.8.cloned.1.call-done = f32[384,2,128]{0,2,1:T(8,128)} async-done(((f32[384,2,128]{0,2,1:T(8,128)}), f32[384,2,128]{0,2,1:T(8,128)}) %all-reduce.8.cloned.1.call-update) | async-done | bytes 393232 | tf_op jit(solution)/shard_map/psum | solution.py:99
  407.7 1.0 multiply_reduce_fusion
  408.8 1.1 multiply_multiply_fusion
  411.8 114.2 %pmax.14 = f32[8,1,2,48]{3,2,0,1:T(2,128)S(1)} all-reduce(f32[8,1,2,48]{3,2,0,1:T(2,128)S(1)} %bitcast.138), channel_id=1, replica_groups=mesh['seq'=64,'tp'=8] {'seq'}, use_global_device_ids=true, to_apply=%region_6.0 | all-reduce | flops 768 | bytes 6144 | tf_op jit(solution)/shard_map/pmax | solution.py:127
  526.5 1.1 fusion.2
  528.0 219.3 %all-reduce.13 = (bf16[384,128]{1,0:T(8,128)(2,1)S(1)}, f32[8,1,2,48]{3,2,0,1:T(2,128)S(1)}) all-reduce(f32[384,128]{1,0:T(8,128)S(1)} %fusion.84, f32[8,1,2,48]{3,2,0,1:T(2,128)S(1)} %get-tuple-element.32), channel_id=1, replica_groups=mesh['seq'=64,'tp'=8] {'seq'}, use_global_device_ids=true, to_apply=%region_11.12 | all-reduce | flops 49920 | bytes 301056 | tf_op jit(solution)/shard_map/psum | solution.py:99
  747.3 74.5 %all-reduce.12.cloned.1.call-done = (f32[8,1,2,48,128]{4,3,2,0,1:T(8,128)}, f32[384,128]{1,0:T(8,128)}, f32[384,256]{1,0:T(8,128)}) async-done(((f32[8,1,2,48,128]{4,3,2,0,1:T(8,128)}, f32[384,128]{1,0:T(8,128)}, f32[384,256]{1,0:T(8,128)}), (f32[8,1,2,48,128]{4,3,2,0,1:T(8,128)}, f32[384,128]{1,0:T(8,128)}, f32[384,256]{1,0:T(8,128)})) %all-reduce.12.cloned.1.call-update) | async-done | bytes 983056 | tf_op jit(solution)/shard_map/psum | solution.py:129
  821.8 1.1 multiply_reduce_fusion.1
  822.9 1.1 multiply_bitcast_fusion
  826.7 39.9 %psum.105 = f32[384,32]{0,1:T(8,128)S(1)} all-reduce(f32[384,32]{0,1:T(8,128)S(1)} %fusion.43), channel_id=1, replica_groups=mesh['seq'=64,'tp'=8] {'tp'}, use_global_device_ids=true, to_apply=%region_16.17 | all-reduce | flops 12288 | bytes 98304 | tf_op jit(solution)/shard_map/psum | solution.py:150
  866.6 110.1 %psum.106 = f32[384]{0:T(512)S(1)} all-reduce(f32[384]{0:T(512)S(1)} %get-tuple-element.21), channel_id=1, replica_groups=mesh['seq'=64,'tp'=8] {'seq'}, use_global_device_ids=true, to_apply=%region_18.19 | all-reduce | flops 384 | bytes 3072 | tf_op jit(solution)/shard_map/psum | solution.py:153
  976.7 1.4 fusion.63
  978.2 1.4 fusion.65
  979.6 295.5 %all-reduce.10.cloned.1.call-done = (f32[384,768]{1,0:T(8,128)}, f32[384,768]{1,0:T(8,128)}) async-done(((f32[384,768]{1,0:T(8,128)}, f32[384,768]{1,0:T(8,128)}), (f32[384,768]{1,0:T(8,128)}, f32[384,768]{1,0:T(8,128)})) %all-reduce.10.cloned.1.call-update) | async-done | bytes 2359312 | tf_op jit(solution)/shard_map/psum | solution.py:157
  1275.1 2.1 fusion.8
  1277.2 30.1 %psum.109 = f32[384,32]{0,1:T(8,128)S(1)} all-reduce(f32[384,32]{0,1:T(8,128)S(1)} %fusion.8), channel_id=1, replica_groups=mesh['seq'=64,'tp'=8] {'tp'}, use_global_device_ids=true, to_apply=%region_21.22 | all-reduce | flops 12288 | bytes 98304 | tf_op jit(solution)/shard_map/psum | solution.py:166
  1307.3 112.8 %psum.110 = f32[384]{0:T(512)S(1)} all-reduce(f32[384]{0:T(512)S(1)} %get-tuple-element.19), channel_id=1, replica_groups=mesh['seq'=64,'tp'=8] {'seq'}, use_global_device_ids=true, to_apply=%region_23.24 | all-reduce | flops 384 | bytes 3072 | tf_op jit(solution)/shard_map/psum | solution.py:169
  1420.2 1.3 stack.2
  1421.5 8.0 all-to-all-start
  1431.1 1.5 gather_fusion
  1432.8 2.6 fusion.1
  1435.4 1.6 fusion
  1436.9 36.7 %all-to-all-done = bf16[64,384,32]{1,2,0:T(8,128)(2,1)S(1)} async-done(((bf16[64,384,32]{1,2,0:T(8,128)(2,1)}), bf16[64,384,32]{1,2,0:T(8,128)(2,1)S(1)}, u32[]{:S(2)}, u32[]{:S(2)}) %all-to-all-start) | async-done | bytes 1572896 | tf_op jit(solution)/shard_map/all_to_all | solution.py:175
  1474.4 136.3 %pmax.15 = f32[384]{0:T(512)S(1)} all-reduce(f32[384]{0:T(512)S(1)} %get-tuple-element.41), channel_id=1, replica_groups=mesh['seq'=64,'tp'=8] {'seq','tp'}, use_global_device_ids=true, to_apply=%region_25.26 | all-reduce | flops 384 | bytes 3072 | tf_op jit(solution)/shard_map/pmax | solution.py:181
  1610.8 99.4 %psum.111 = f32[384]{0:T(512)S(1)} all-reduce(f32[384]{0:T(512)S(1)} %exponential_reduce_fusion), channel_id=1, replica_groups=mesh['seq'=64,'tp'=8] {'seq','tp'}, use_global_device_ids=true, to_apply=%region_27.28 | all-reduce | flops 384 | bytes 3072 | tf_op jit(solution)/shard_map/psum | solution.py:182
  1710.2 0.9 copy.36
  (100 shorter events, 10.5 us)
Async XLA Ops:
  7.2 1466.5 %copy-start = (bf16[2048,256]{1,0:T(8,128)(2,1)S(1)}, bf16[2048,256]{1,0:T(8,128)(2,1)}, u32[]{:S(2)}) copy-start(bf16[2048,256]{1,0:T(8,128)(2,1)} %param.35) | copy-start | bytes 3145732
  7.2 400.6 %all-reduce.8.cloned.1.call-start = ((), (), s32[]{:S(2)}) async-start(), calls=%async_computation.1 | async-start | bytes 786432 | tf_op jit(solution)/shard_map/psum | solution.py:99
  132.7 689.1 %all-reduce.12.cloned.1.call-start = ((), (), s32[]{:S(2)}) async-start(), calls=%async_computation.3 | async-start | bytes 1966080 | tf_op jit(solution)/shard_map/psum | solution.py:129
  134.6 1.4 copy-start.12
  134.6 1.6 copy-start.1
  134.6 1.6 copy-start.8
  134.6 1.6 copy-start.9
  135.0 2.7 copy-start.7
  135.3 273.5 %copy-start.16 = (f32[128]{0:T(128)S(1)}, f32[128]{0:T(128)}, u32[]{:S(2)}) copy-start(f32[128]{0:T(128)} %param.27) | copy-start | bytes 1540
  410.4 1.0 copy-start.2
  411.4 115.0 %copy-start.3 = (bf16[8,256,128]{2,1,0:T(8,128)(2,1)S(1)}, bf16[8,256,128]{2,1,0:T(8,128)(2,1)}, u32[]{:S(2)}) copy-start(bf16[8,256,128]{2,1,0:T(8,128)(2,1)} %param.38) | copy-start | bytes 1572868
  526.5 1.2 copy-start.10
  527.5 295.3 %copy-start.13 = (f32[128]{0:T(128)S(1)}, f32[128]{0:T(128)}, u32[]{:S(2)}) copy-start(f32[128]{0:T(128)} %param.28) | copy-start | bytes 1540
  527.6 747.5 %all-reduce.10.cloned.1.call-start = ((), (), s32[]{:S(2)}) async-start(), calls=%async_computation.2 | async-start | bytes 4718592 | tf_op jit(solution)/shard_map/psum | solution.py:157
  747.3 79.3 %copy-start.19 = (bf16[384,128]{1,0:T(8,128)(2,1)}, bf16[384,128]{1,0:T(8,128)(2,1)S(1)}, u32[]{:S(2)}) copy-start(bf16[384,128]{1,0:T(8,128)(2,1)S(1)} %get-tuple-element.12) | copy-start | bytes 294916
  822.9 2.5 copy-start.18
  825.4 1.0 copy-start.17
  825.4 1.0 copy-start.21
  826.0 150.7 %copy-start.5 = (bf16[32,768]{1,0:T(8,128)(2,1)S(1)}, bf16[32,768]{1,0:T(8,128)(2,1)}, u32[]{:S(2)}) copy-start(bf16[32,768]{1,0:T(8,128)(2,1)} %param.32) | copy-start | bytes 147460
  826.0 150.7 %copy-start.11 = (f32[32]{0:T(128)S(1)}, f32[32]{0:T(128)}, u32[]{:S(2)}) copy-start(f32[32]{0:T(128)} %param.30) | copy-start | bytes 388
  826.7 151.5 %copy-start.6 = (bf16[32,768]{1,0:T(8,128)(2,1)S(1)}, bf16[32,768]{1,0:T(8,128)(2,1)}, u32[]{:S(2)}) copy-start(bf16[32,768]{1,0:T(8,128)(2,1)} %param.31) | copy-start | bytes 147460
  979.6 295.5 %copy-start.20 = (bf16[768,32]{0,1:T(8,128)(2,1)S(1)}, bf16[768,32]{0,1:T(8,128)(2,1)}, u32[]{:S(2)}) copy-start(bf16[768,32]{0,1:T(8,128)(2,1)} %param.33) | copy-start | bytes 147460
  1275.1 145.0 %copy-start.14 = (f32[32]{0:T(128)S(1)}, f32[32]{0:T(128)}, u32[]{:S(2)}) copy-start(f32[32]{0:T(128)} %param.34) | copy-start | bytes 388
  1307.3 114.2 %copy-start.4 = (bf16[384,32]{0,1:T(8,128)(2,1)}, bf16[384,32]{0,1:T(8,128)(2,1)S(1)}, u32[]{:S(2)}) copy-start(bf16[384,32]{0,1:T(8,128)(2,1)S(1)} %get-tuple-element.20) | copy-start | bytes 73732
  1421.5 8.0 copy-start.15
  1421.5 52.2 %all-to-all-start = ((bf16[64,384,32]{1,2,0:T(8,128)(2,1)}), bf16[64,384,32]{1,2,0:T(8,128)(2,1)S(1)}, u32[]{:S(2)}, u32[]{:S(2)}) async-start(bf16[64,384,32]{1,2,0:T(8,128)(2,1)} %stack.2), calls=%async_computation | async-start | bytes 3145728 | tf_op jit(solution)/shard_map/all_to_all | solution.py:175
Sparse Core Ops, SparseCore 0:
  132.9 274.8 all-reduce.7
  527.7 294.0 all-reduce.11
  979.7 295.3 all-reduce.9
